TPU v7x, 256 devices: a whole 4x4x8 slice. The times are simulated.
256 devices in a mesh: seq: 16 (over z, x_lo), wr: 4 (over y), wc: 4 (over x_hi, core).
Axes of the slice: x: 4 (x_hi: 2, x_lo: 2; x = x_hi * 2 + x_lo), y: 4, z: 8, core: 2. Of those that a mesh axis runs over, the one named last changes fastest.
Arguments:
- tokens: bfloat16 [8192, 2048], P('seq', ('wr', 'wc')), may hold values from -6 to 6
- ln_gain: float32 [2, 2048], replicated, may hold values from 0.5 to 1.5
- w_branch: bfloat16 [2, 2048, 4096], P(None, None, ('wr', 'wc')), may hold values from -0.125 to 0.125
- w_outgate: bfloat16 [2, 2048, 4096], P(None, None, ('wr', 'wc')), may hold values from -0.125 to 0.125
- w_gates: bfloat16 [2, 2048, 8], replicated, may hold values from -0.125 to 0.125
- forget_bias: float32 [2, 4], replicated, may hold values from 3.2 to 11
- conv_weight: float32 [2, 4, 4096], P(None, None, ('wr', 'wc')), may hold values from -3 to 3
- conv_bias: float32 [2, 4096], P(None, ('wr', 'wc')), may hold values from -3 to 3
- w_query: float32 [2, 4, 4, 4, 256], P(None, 'wr'), may hold values from -3 to 3
- w_key: float32 [2, 4, 4, 4, 256], P(None, 'wr'), may hold values from -3 to 3
- w_value: float32 [2, 4, 4, 4, 256], P(None, 'wr', None, 'wc'), may hold values from -4 to 4
- skip_gain: float32 [2, 4096], P(None, ('wr', 'wc')), may hold values from 0.5 to 1.5
- norm_gain: float32 [2, 4096], P(None, ('wr', 'wc')), may hold values from 0.5 to 1.5
- w_down: bfloat16 [2, 4096, 2048], P(None, ('wr', 'wc')), may hold values from -0.125 to 0.125
- lengths: int32 [3], replicated, may hold values from 1 to 4096, 8192 in all
- request_prompt: int32 [32], P('seq'), may hold values from 0 to 2
Outputs:
- mixed: bfloat16 [8192, 2048], P('seq', ('wr', 'wc'))
- request_state: bfloat16 [2, 32, 4, 1024, 1024], P(None, 'seq', 'wr', None, 'wc')
- request_conv: bfloat16 [2, 32, 3, 4096], P(None, 'seq', None, ('wr', 'wc'))
Inputs may be any that keep to these rules, and one draw needn't show every extreme that they name: `lengths`: the 3 prompts lie end to end in order and fill all 8192 positions; the longest has exactly 4096 positions.
All inputs are finite; a program needn't handle non-finite values.
Results may differ from a plain program's by a relative error of at most 0.035.
Values may be sent and summed in bfloat16 or wider, within the bound.
A program may use at most 128 MiB of HBM per device.

v0:
```python
import jax
import jax.numpy as jnp
from jax import lax
from jax.sharding import PartitionSpec as P

HEADS = 4
CONV = 4
LAYERS = 2
PROMPTS = 3
EPSILON = 1e-05
GATE_CAP = 15.0
ROW_DIMS = (((0,), (0,)), ((), ()))
FEATURE_DIMS = (((1,), (1,)), ((), ()))


def shifted(value, axis, steps):
    count = lax.axis_size(axis)
    first, last = (max(0, -steps), min(count, count - steps))
    return lax.ppermute(value, axis, [(source, source + steps) for source in range(first, last)])


def entering_2(shard, axis, join, neutral):
    place = lax.axis_index(axis)
    gathered = jax.tree.map(
        lambda a, kind: lax.all_gather(a.astype(kind), axis), shard, (jnp.bfloat16, jnp.bfloat16)
    )
    state = jax.tree.map(lambda a, e: jnp.zeros_like(a) + jnp.asarray(e, a.dtype), shard, neutral)

    def one(step, state):
        return join(
            state,
            jax.tree.map(
                lambda a, own: lax.dynamic_index_in_dim(a, step, 0, False).astype(own.dtype),
                gathered,
                shard,
            ),
        )

    return lax.fori_loop(0, place, one, state)


def broadcast(shard, axis, root):
    mine = lax.axis_index(axis) == root
    return lax.psum(jnp.where(mine, shard, jnp.zeros_like(shard)), axis)


def norm_rows(source, gain_row):
    widened = source.astype(jnp.float32)
    row_mean = jnp.mean(widened, axis=1, keepdims=True)
    row_var = jnp.mean(widened * widened, axis=1, keepdims=True) - row_mean * row_mean
    return ((widened - row_mean) * lax.rsqrt(row_var + EPSILON) * gain_row).astype(jnp.bfloat16)


def segment_of(positions, lengths):
    bound_one = lengths[0]
    bound_two = lengths[0] + lengths[1]
    return (positions >= bound_one).astype(jnp.int32) + (positions >= bound_two).astype(jnp.int32)


def conv_rows(extended, ext_segment, segment, weight, bias_row):
    row_count = segment.shape[0]
    widened = extended.astype(jnp.float32)
    summed = jnp.zeros((row_count, widened.shape[1]), jnp.float32) + bias_row
    for back_step in range(weight.shape[0]):
        low_row = weight.shape[0] - 1 - back_step
        keep_row = (ext_segment[low_row : low_row + row_count] == segment).astype(jnp.float32)
        summed = (
            summed + weight[back_step] * widened[low_row : low_row + row_count] * keep_row[:, None]
        )
    return jax.nn.silu(summed).astype(jnp.bfloat16)


def block_mix(source, weight):
    row_count = source.shape[0]
    grouped = source.astype(jnp.float32).reshape(row_count, 4, -1)
    mixed = jnp.einsum("tig,ijg->tjg", grouped, weight, precision=lax.Precision.HIGHEST)
    return mixed.reshape(row_count, -1)


def block_terms(queries, key_rows, values, log_forget, in_gate, segment, prev_seg):
    row_count = queries.shape[0]
    cum_log = jnp.cumsum(log_forget)
    row_order = jnp.arange(row_count)
    allowed = (row_order[:, None] >= row_order[None, :]) & (segment[:, None] == segment[None, :])
    exponent = jnp.where(allowed, cum_log[:, None] - cum_log[None, :] + in_gate[None, :], -jnp.inf)
    scores = lax.dot_general(
        queries, key_rows, FEATURE_DIMS, preferred_element_type=jnp.float32
    ) * jnp.exp(exponent)
    in_block = jnp.dot(scores.astype(jnp.bfloat16), values, preferred_element_type=jnp.float32)
    carried = jnp.where(segment == prev_seg, jnp.exp(cum_log), 0.0)
    last_seg = segment[row_count - 1]
    weights = jnp.where(
        segment == last_seg, jnp.exp(cum_log[row_count - 1] - cum_log + in_gate), 0.0
    )
    weighted = (key_rows.astype(jnp.float32) * weights[:, None]).astype(jnp.bfloat16)
    increment = lax.dot_general(weighted, values, ROW_DIMS, preferred_element_type=jnp.float32)
    block_decay = jnp.where(last_seg == prev_seg, jnp.exp(cum_log[row_count - 1]), 0.0)
    return (in_block, carried, increment, block_decay)


def end_state(
    state_in, key_rows, values, cum_log, in_gate, segment, seg_before, local_end, prompt, holder
):
    end_cum = cum_log[local_end]
    entering = jnp.where(holder & (seg_before == prompt), jnp.exp(end_cum), 0.0)
    row_order = jnp.arange(segment.shape[0])
    chosen = holder & (segment == prompt) & (row_order <= local_end)
    weights = jnp.where(chosen, jnp.exp(end_cum - cum_log + in_gate), 0.0)
    weighted = (key_rows.astype(jnp.float32) * weights[:, None]).astype(jnp.bfloat16)
    return entering * state_in + lax.dot_general(
        weighted, values, ROW_DIMS, preferred_element_type=jnp.float32
    )


def combine_states(earlier, later):
    return (earlier[0] * later[0], later[0] * earlier[1] + later[1])


def body(
    tokens,
    ln_gain,
    w_branch,
    w_outgate,
    w_gates,
    forget_bias,
    conv_weight,
    conv_bias,
    w_query,
    w_key,
    w_value,
    skip_gain,
    norm_gain,
    w_down,
    lengths,
    request_prompt,
):
    tok_rows = tokens.shape[0]
    seq_count = lax.axis_size("seq")
    seq_index = lax.axis_index("seq")
    head_idx = lax.axis_index("wr")
    row_offset = seq_index * tok_rows
    total_rows = tok_rows * seq_count
    row_ids = jnp.arange(tok_rows, dtype=jnp.int32)
    positions = row_offset + row_ids
    segment = segment_of(positions, lengths)
    seg_before = jnp.where(row_offset > 0, segment_of(row_offset - 1, lengths), -1)
    rim_positions = row_offset - (CONV - 1) + jnp.arange(CONV - 1, dtype=jnp.int32)
    rim_segment = jnp.where(rim_positions >= 0, segment_of(rim_positions, lengths), -1)
    ext_segment = jnp.concatenate([rim_segment, segment])
    prompt_starts = [jnp.zeros((), jnp.int32), lengths[0], lengths[0] + lengths[1]]
    prompt_ends = [
        lengths[0] - 1,
        lengths[0] + lengths[1] - 1,
        jnp.zeros((), jnp.int32) + (total_rows - 1),
    ]
    head_mask = (jnp.arange(HEADS, dtype=jnp.int32) == head_idx).astype(jnp.float32)
    current = tokens
    sent_states = []
    sent_edges = []
    for layer_idx in range(LAYERS):
        gathered = lax.all_gather(current, ("wr", "wc"), axis=1, tiled=True)
        normed = norm_rows(gathered, ln_gain[layer_idx])
        branch = jnp.dot(normed, w_branch[layer_idx], preferred_element_type=jnp.float32).astype(
            jnp.bfloat16
        )
        outgate = jnp.dot(normed, w_outgate[layer_idx], preferred_element_type=jnp.float32)
        gate_pre = jnp.dot(normed, w_gates[layer_idx], preferred_element_type=jnp.float32)
        input_pre = jnp.sum(gate_pre[:, :HEADS] * head_mask, axis=1)
        forget_pre = jnp.sum((gate_pre[:, HEADS:] + forget_bias[layer_idx]) * head_mask, axis=1)
        in_gate = GATE_CAP * jnp.tanh(input_pre / GATE_CAP)
        log_forget = jax.nn.log_sigmoid(forget_pre)
        edge_in = shifted(branch[tok_rows - (CONV - 1) :], "seq", 1)
        extended = jnp.concatenate([edge_in, branch], axis=0)
        conv_act = conv_rows(
            extended, ext_segment, segment, conv_weight[layer_idx], conv_bias[layer_idx]
        )
        head_branch, head_act = (
            lax.all_gather(branch, "wc", axis=1, tiled=True),
            lax.all_gather(conv_act, "wc", axis=1, tiled=True),
        )
        head_width = head_act.shape[1]
        queries = block_mix(head_act, w_query[layer_idx, 0]).astype(jnp.bfloat16)
        key_rows = (block_mix(head_act, w_key[layer_idx, 0]) * head_width ** (-0.5)).astype(
            jnp.bfloat16
        )
        values = block_mix(head_branch, w_value[layer_idx, 0]).astype(jnp.bfloat16)
        prefix = jnp.zeros((head_width, values.shape[1]), jnp.float32)
        reach_all = jnp.ones((), jnp.float32)
        in_block, carried, increment, block_decay = block_terms(
            queries, key_rows, values, log_forget, in_gate, segment, seg_before
        )
        saved_parts = (in_block, carried, reach_all, prefix)
        prefix = block_decay * prefix + increment
        reach_all = block_decay * reach_all
        entering = entering_2(
            (reach_all, prefix),
            "seq",
            combine_states,
            (jnp.ones((), jnp.float32), jnp.zeros_like(prefix)),
        )[1]
        in_block, carried, reach_here, prefix_here = saved_parts
        state_here = (reach_here * entering + prefix_here).astype(jnp.bfloat16)
        hidden_parts = in_block + carried[:, None] * jnp.dot(
            queries, state_here, preferred_element_type=jnp.float32
        )
        sums_one, sums_two = lax.psum(
            (jnp.sum(hidden_parts, axis=1), jnp.sum(hidden_parts * hidden_parts, axis=1)), "wc"
        )
        row_mean = sums_one / head_width
        row_var = sums_two / head_width - row_mean * row_mean
        normal_rows = (hidden_parts - row_mean[:, None]) * lax.rsqrt(row_var + EPSILON)[:, None]
        gated = (
            (
                normal_rows * norm_gain[layer_idx]
                + skip_gain[layer_idx] * conv_act.astype(jnp.float32)
            )
            * jax.nn.silu(outgate)
        ).astype(jnp.bfloat16)
        term_rows = jnp.dot(gated, w_down[layer_idx], preferred_element_type=jnp.float32)
        summed = lax.psum_scatter(
            term_rows.astype(jnp.bfloat16), ("wr", "wc"), scatter_dimension=1, tiled=True
        ).astype(jnp.float32)
        current = (current.astype(jnp.float32) + summed).astype(jnp.bfloat16)
        cum_log = jnp.cumsum(log_forget)
        for prompt in range(PROMPTS):
            end_pos = prompt_ends[prompt]
            holder = (end_pos >= row_offset) & (end_pos < row_offset + tok_rows)
            local_end = jnp.clip(end_pos - row_offset, 0, tok_rows - 1)
            state_end = end_state(
                entering,
                key_rows,
                values,
                cum_log,
                in_gate,
                segment,
                seg_before,
                local_end,
                prompt,
                holder,
            )
            window = lax.dynamic_slice_in_dim(extended, local_end + 1, CONV - 1, 0)
            edge_pos = end_pos - (CONV - 2) + jnp.arange(CONV - 1, dtype=jnp.int32)
            edge_rows = jnp.where(
                ((edge_pos >= prompt_starts[prompt]) & holder)[:, None],
                window,
                jnp.zeros_like(window),
            )
            got_state, got_edge = (
                broadcast(state_end.astype(jnp.bfloat16), "seq", end_pos // tok_rows),
                broadcast(edge_rows, "seq", end_pos // tok_rows),
            )
            sent_states.append(got_state)
            sent_edges.append(got_edge)
    state_stack = jnp.stack(sent_states)
    edge_stack = jnp.stack(sent_edges)
    state_stack = state_stack.reshape(LAYERS, PROMPTS, state_stack.shape[1], state_stack.shape[2])
    edge_stack = edge_stack.reshape(LAYERS, PROMPTS, edge_stack.shape[1], edge_stack.shape[2])
    chooser = (request_prompt[:, None] == jnp.arange(PROMPTS, dtype=jnp.int32)[None, :]).astype(
        jnp.bfloat16
    )
    request_state = jnp.einsum(
        "rp,lphd->lrhd", chooser, state_stack, preferred_element_type=jnp.float32
    ).astype(jnp.bfloat16)[:, :, None]
    request_conv = jnp.einsum(
        "rp,lpkc->lrkc", chooser, edge_stack, preferred_element_type=jnp.float32
    ).astype(jnp.bfloat16)
    return (current, request_state, request_conv)


def solution(mesh):
    return jax.shard_map(
        body,
        mesh=mesh,
        in_specs=(
            P("seq", ("wr", "wc")),
            P(),
            P(None, None, ("wr", "wc")),
            P(None, None, ("wr", "wc")),
            P(),
            P(),
            P(None, None, ("wr", "wc")),
            P(None, ("wr", "wc")),
            P(None, "wr", None, None, None),
            P(None, "wr", None, None, None),
            P(None, "wr", None, "wc", None),
            P(None, ("wr", "wc")),
            P(None, ("wr", "wc")),
            P(None, ("wr", "wc"), None),
            P(),
            P("seq"),
        ),
        out_specs=(
            P("seq", ("wr", "wc")),
            P(None, "seq", "wr", None, "wc"),
            P(None, "seq", None, ("wr", "wc")),
        ),
        check_vma=False,
    )
```

profile of v0, /device:TPU:8, one launch (start us, length us, event | category | flops | bytes accessed | tf_op | source)
XLA Modules:
  0.0 1085.9 jit_solution(4009449505985787538)
XLA Ops:
  17.0 47.1 %all-gather.11.cloned.1.call-done = bf16[512,2048]{1,0:T(8,128)(2,1)} async-done(((bf16[512,128]{1,0:T(8,128)(2,1)}), bf16[512,2048]{1,0:T(8,128)(2,1)}) %all-gather.11.cloned.1.call-update) | async-done | bytes 2097168 | tf_op jit(solution)/shard_map/all_gather | solution.py:161
  83.8 8.9 all-gather.15.cloned.1.call-done
  97.7 19.7 %all-gather.13.cloned.1.call-done = bf16[512,1024]{1,0:T(8,128)(2,1)} async-done(((bf16[512,256]{1,0:T(8,128)(2,1)}), bf16[512,1024]{1,0:T(8,128)(2,1)}) %all-gather.13.cloned.1.call-update) | async-done | bytes 1048592 | tf_op jit(solution)/shard_map/all_gather | solution.py:179
  122.8 4.2 fusion.99
  144.2 38.1 %all-reduce = bf16[16]{0:T(256)(128)(2,1)S(1)} all-reduce(bf16[16]{0:T(256)(128)(2,1)} %dynamic-update-slice), channel_id=1, replica_groups=mesh['seq'=16,'wr'=4,'wc'=4] {'seq'}, use_global_device_ids=true, to_apply=%add | all-reduce | flops 16 | bytes 64
  187.8 3.2 fusion.53
  191.0 130.3 %all-gather.23.cloned.1.call-done = bf16[16384,256]{1,0:T(8,128)(2,1)} async-done(((bf16[1024,256]{1,0:T(8,128)(2,1)}), bf16[16384,256]{1,0:T(8,128)(2,1)}) %all-gather.23.cloned.1.call-update) | async-done | bytes 8388624 | tf_op jit(solution)/shard_map/all_gather | solution.py:25
  324.8 9.4 all-reduce.3
  334.9 5.5 convolution_convert_fusion.1
  340.4 3.9 copy.136
  344.4 114.9 %reduce-scatter.7.cloned.1.call-done = bf16[128,512]{1,0:T(8,128)(2,1)} async-done(((bf16[2048,512]{1,0:T(8,128)(2,1)}), bf16[128,512]{1,0:T(8,128)(2,1)}) %reduce-scatter.7.cloned.1.call-update) | async-done | bytes 131088
  461.1 51.2 %all-gather.17.cloned.1.call-done = bf16[512,2048]{1,0:T(8,128)(2,1)} async-done(((bf16[512,128]{1,0:T(8,128)(2,1)}), bf16[512,2048]{1,0:T(8,128)(2,1)}) %all-gather.17.cloned.1.call-update) | async-done | bytes 2097168 | tf_op jit(solution)/shard_map/all_gather | solution.py:161
  532.5 8.4 all-gather.21.cloned.1.call-done
  545.0 20.6 %all-gather.19.cloned.1.call-done = bf16[512,1024]{1,0:T(8,128)(2,1)} async-done(((bf16[512,256]{1,0:T(8,128)(2,1)}), bf16[512,1024]{1,0:T(8,128)(2,1)}) %all-gather.19.cloned.1.call-update) | async-done | bytes 1048592 | tf_op jit(solution)/shard_map/all_gather | solution.py:179
  568.9 4.2 fusion.96
  590.7 71.5 %all-reduce.4 = (bf16[16]{0:T(256)(128)(2,1)S(1)}, bf16[1,3,256]{2,1,0:T(4,128)(2,1)S(1)}, bf16[1,3,256]{2,1,0:T(4,128)(2,1)S(1)}, bf16[1,3,256]{2,1,0:T(4,128)(...) all-reduce(bf16[16]{0:T(256)(128)(2,1)S(1)} %dynamic-update-slice.1, ...), channel_id=1, replica_groups=mesh['seq'=16,'wr'=4,'wc'=4] {'seq'}, use_global_device_ids=true, to_apply=%add.1 | all-reduce | flops 4624 | bytes 18496
  667.5 3.3 fusion.52
  670.8 99.3 %all-gather.25.cloned.1.call-done = bf16[16384,256]{1,0:T(8,128)(2,1)} async-done(((bf16[1024,256]{1,0:T(8,128)(2,1)}), bf16[16384,256]{1,0:T(8,128)(2,1)}) %all-gather.25.cloned.1.call-update) | async-done | bytes 8388624 | tf_op jit(solution)/shard_map/all_gather | solution.py:25
  773.1 8.8 all-reduce.2
  782.0 6.1 convolution_convert_fusion
  788.1 3.9 copy.138
  798.1 3.4 fusion.19
  823.8 82.0 %reduce-scatter.9.cloned.1.call-done = bf16[128,512]{1,0:T(8,128)(2,1)} async-done(((bf16[2048,512]{1,0:T(8,128)(2,1)}), bf16[128,512]{1,0:T(8,128)(2,1)}) %reduce-scatter.9.cloned.1.call-update) | async-done | bytes 131088
  907.5 164.3 %all-reduce.8.cloned.1.call-done = (bf16[1,1024,256]{2,1,0:T(8,128)(2,1)}, bf16[1,1024,256]{2,1,0:T(8,128)(2,1)}, bf16[1,1024,256]{2,1,0:T(8,128)(2,1)}, bf16[1,...) async-done(((bf16[1,1024,256]{2,1,0:T(8,128)(2,1)}, bf16[1,1024,256]{2,1,0:T(8,128)(2,1)}, bf16[1,1024,256]{2,1,0:T(8,128)(2,1)}, ...) | async-done | bytes 3145744 | tf_op jit(solution)/shard_map/psum | solution.py:44
  (254 shorter events, 149.1 us)
Async XLA Ops:
  7.2 56.9 %all-gather.11.cloned.1.call-start = ((), (), s32[]{:S(2)}) async-start(), calls=%async_computation.2 | async-start | bytes 2228224 | tf_op jit(solution)/shard_map/all_gather | solution.py:161
  7.9 84.8 %all-gather.15.cloned.1.call-start = ((), (), s32[]{:S(2)}) async-start(), calls=%async_computation.4 | async-start | bytes 1310720 | tf_op jit(solution)/shard_map/all_gather | solution.py:178
  11.3 59.7 %copy-start.39 = (f32[4]{0:T(128)}, f32[4]{0:T(128)S(1)}, u32[]{:S(2)}) copy-start(f32[4]{0:T(128)S(1)} %compare_convert_fusion) | copy-start | bytes 52
  69.6 47.8 %all-gather.13.cloned.1.call-start = ((), (), s32[]{:S(2)}) async-start(), calls=%async_computation.3 | async-start | bytes 1310720 | tf_op jit(solution)/shard_map/all_gather | solution.py:179
  71.0 7.3 copy-start.23
  71.1 10.8 copy-start.24
  71.5 4.1 collective-permute-start
  75.5 8.3 copy-start.30
  75.7 8.1 copy-start.27
  76.9 244.4 %all-gather.23.cloned.1.call-start = ((), (), s32[]{:S(2)}) async-start(), calls=%async_computation.8 | async-start | bytes 8912896 | tf_op jit(solution)/shard_map/all_gather | solution.py:25
  138.0 321.3 %reduce-scatter.7.cloned.1.call-start = ((), (), s32[]{:S(2)}) async-start(), calls=%async_computation.10 | async-start | bytes 2228224
  344.3 116.0 %copy-start.17 = (bf16[512,128]{1,0:T(8,128)(2,1)S(1)}, bf16[512,128]{1,0:T(8,128)(2,1)}, u32[]{:S(2)}) copy-start(bf16[512,128]{1,0:T(8,128)(2,1)} %param.20) | copy-start | bytes 393220
  344.3 168.0 %all-gather.17.cloned.1.call-start = ((), (), s32[]{:S(2)}) async-start(), calls=%async_computation.5 | async-start | bytes 2228224 | tf_op jit(solution)/shard_map/all_gather | solution.py:161
  461.0 79.9 %all-gather.21.cloned.1.call-start = ((), (), s32[]{:S(2)}) async-start(), calls=%async_computation.7 | async-start | bytes 1310720 | tf_op jit(solution)/shard_map/all_gather | solution.py:178
  516.4 10.1 copy-start
  517.8 7.6 copy-start.26
  517.8 47.8 %all-gather.19.cloned.1.call-start = ((), (), s32[]{:S(2)}) async-start(), calls=%async_computation.6 | async-start | bytes 1310720 | tf_op jit(solution)/shard_map/all_gather | solution.py:179
  518.6 3.8 collective-permute-start.1
  525.2 244.9 %all-gather.25.cloned.1.call-start = ((), (), s32[]{:S(2)}) async-start(), calls=%async_computation.9 | async-start | bytes 8912896 | tf_op jit(solution)/shard_map/all_gather | solution.py:25
  585.6 320.2 %reduce-scatter.9.cloned.1.call-start = ((), (), s32[]{:S(2)}) async-start(), calls=%async_computation.11 | async-start | bytes 2228224
  770.4 11.5 %copy-start.44 = (f32[1,256]{1,0:T(1,128)S(1)}, f32[1,256]{1,0:T(1,128)}, u32[]{:S(2)}) copy-start(f32[1,256]{1,0:T(1,128)} %get-tuple-element.222) | copy-start | bytes 3076
  770.4 11.5 %copy-start.45 = (f32[1,256]{1,0:T(1,128)S(1)}, f32[1,256]{1,0:T(1,128)}, u32[]{:S(2)}) copy-start(f32[1,256]{1,0:T(1,128)} %get-tuple-element.220) | copy-start | bytes 3076
  792.0 279.8 %all-reduce.8.cloned.1.call-start = ((), (), s32[]{:S(2)}) async-start(), calls=%async_computation.12 | async-start | bytes 6291456 | tf_op jit(solution)/shard_map/psum | solution.py:44
  822.3 84.5 %copy-start.16 = (bf16[512,128]{1,0:T(8,128)(2,1)S(1)}, bf16[512,128]{1,0:T(8,128)(2,1)}, u32[]{:S(2)}) copy-start(bf16[512,128]{1,0:T(8,128)(2,1)} %add_convert_fusion.1) | copy-start | bytes 393220
  (39 other events, 125.7 us)
Sparse Core Ops, SparseCore 0:
  10.6 53.4 all-gather.10
  69.7 22.9 all-gather.14
  94.5 22.8 all-gather.12
  138.1 183.1 all-gather.22
  344.4 114.8 reduce-scatter.6
  462.3 49.9 all-gather.16
  518.0 22.8 all-gather.20
  542.7 22.8 all-gather.18
  585.7 184.3 all-gather.24
  792.1 113.6 reduce-scatter.8
  908.9 162.8 all-reduce.7
where the time goes:
time: 1100 us; the launch traced here: 1090 us
  waiting for transfers between devices  749 us (68%)
  blocking collectives  128 us (12%)
  local copies, waits for them, and re-layouts  79.5 us (7%)
  matrix products  59.7 us (5%)
  other arithmetic  39.7 us (4%)
  between operations  24.4 us (2%)
    all_gather x2, waiting for transfers between devices, entering_2(): lax.all_gather(a.astype(kind), axis)  230 us
    unnamed x13, waiting for transfers between devices  198 us
    psum x1, waiting for transfers between devices, broadcast(): return lax.psum(jnp.where(mine, shard, jnp.zeros_like(shard)), axis)  164 us
    unnamed x2, blocking collectives  110 us
    all_gather x2, waiting for transfers between devices, body(): gathered = lax.all_gather(current, ('wr', 'wc'), axis=1, tiled=True)  98.3 us
    all_gather x2, waiting for transfers between devices, body(): lax.all_gather(conv_act, 'wc', axis=1, tiled=True)  40.3 us
    unnamed x126, local copies, waits for them, and re-layouts  27.7 us
  transfers between devices with their start and end apart: 13, of which 12 were waited for; matrix products, arithmetic and copies ran while one was open for 8% of the time, Pallas kernels for 0%

commit v1 on v0

--- a/solution.py
+++ b/solution.py
@@ -158,7 +158,10 @@
     sent_states = []
     sent_edges = []
     for layer_idx in range(LAYERS):
-        gathered = lax.all_gather(current, ("wr", "wc"), axis=1, tiled=True)
+        arr_next = tuple((current for _ in range(lax.axis_size(("wr", "wc")))))
+        response = jnp.stack(arr_next, 0)
+        inter = lax.all_to_all(response, ("wr", "wc"), 0, 0)
+        gathered = jnp.concatenate(inter, 1)
         normed = norm_rows(gathered, ln_gain[layer_idx])
         branch = jnp.dot(normed, w_branch[layer_idx], preferred_element_type=jnp.float32).astype(
             jnp.bfloat16

time: 1100 us -> 1050 us (0.955)
  waiting for transfers between devices: 749 us -> 669 us
  blocking collectives: 128 us -> 159 us
    all_gather x2 -> x0, waiting for transfers between devices: 98.3 us -> none  [body(): gathered = lax.all_gather(current, ('wr', 'wc'), axis=1, tiled=True)]
    all_to_all x0 -> x1, blocking collectives: none -> 31.8 us  [body(): inter = lax.all_to_all(response, ('wr', 'wc'), 0, 0)]
    all_to_all x0 -> x1, waiting for transfers between devices: none -> 20.9 us  [body(): inter = lax.all_to_all(response, ('wr', 'wc'), 0, 0)]
    unnamed x126 -> x173, local copies, waits for them, and re-layouts: 27.7 us -> 31.2 us
    unnamed x13 -> x11, waiting for transfers between devices: 198 us -> 199 us
  transfers between devices with their start and end apart: 13 -> 12, of which waited for: 12 -> 12; matrix products, arithmetic and copies ran while one was open for 8% -> 9% of each run, Pallas kernels for 0% -> 0%
where the time goes in v1:
time: 1050 us; the launch traced here: 1040 us
  waiting for transfers between devices  669 us (64%)
  blocking collectives  159 us (15%)
  local copies, waits for them, and re-layouts  75.9 us (7%)
  matrix products  59.2 us (6%)
  other arithmetic  34.9 us (3%)
  between operations  24.3 us (2%)
  starting transfers between devices  14.3 us (1%)
    all_gather x2, waiting for transfers between devices, entering_2(): lax.all_gather(a.astype(kind), axis)  232 us
    unnamed x11, waiting for transfers between devices  199 us
    psum x1, waiting for transfers between devices, broadcast(): return lax.psum(jnp.where(mine, shard, jnp.zeros_like(shard)), axis)  164 us
    unnamed x2, blocking collectives  110 us
    all_gather x2, waiting for transfers between devices, body(): lax.all_gather(conv_act, 'wc', axis=1, tiled=True)  41.7 us
    all_to_all x1, blocking collectives, body(): inter = lax.all_to_all(response, ('wr', 'wc'), 0, 0)  31.8 us
    unnamed x173, local copies, waits for them, and re-layouts  31.2 us
  transfers between devices with their start and end apart: 12, of which 12 were waited for; matrix products, arithmetic and copies ran while one was open for 9% of the time, Pallas kernels for 0%

profile of v1, /device:TPU:8, one launch (start us, length us, event | category | flops | bytes accessed | tf_op | source)
XLA Modules:
  0.0 1037.3 jit_solution(14330611421056700775)
XLA Ops:
  9.7 7.5 all-to-all-start
  23.0 20.9 %all-to-all-done = bf16[16,512,128]{1,2,0:T(8,128)(2,1)S(1)} async-done(((bf16[16,512,128]{1,2,0:T(8,128)(2,1)}), bf16[16,512,128]{1,2,0:T(8,128)(2,1)S(1)}, u32[]{:S(2)}, u32[]{:S(2)}) %all-to-all-start) | async-done | bytes 2097184 | tf_op jit(solution)/shard_map/all_to_all | solution.py:163
  51.3 3.7 collective-permute-start
  64.5 8.3 all-gather.11.cloned.1.call-done
  76.2 21.3 %all-gather.9.cloned.1.call-done = bf16[512,1024]{1,0:T(8,128)(2,1)} async-done(((bf16[512,256]{1,0:T(8,128)(2,1)}), bf16[512,1024]{1,0:T(8,128)(2,1)}) %all-gather.9.cloned.1.call-update) | async-done | bytes 1048592 | tf_op jit(solution)/shard_map/all_gather | solution.py:182
  115.0 39.9 %all-reduce = bf16[16]{0:T(256)(128)(2,1)S(1)} all-reduce(bf16[16]{0:T(256)(128)(2,1)S(1)} %dynamic-update-slice), channel_id=1, replica_groups=mesh['seq'=16,'wr'=4,'wc'=4] {'seq'}, use_global_device_ids=true, to_apply=%add | all-reduce | flops 16 | bytes 64
  160.9 133.5 %all-gather.17.cloned.1.call-done = bf16[16384,256]{1,0:T(8,128)(2,1)} async-done(((bf16[1024,256]{1,0:T(8,128)(2,1)}), bf16[16384,256]{1,0:T(8,128)(2,1)}) %all-gather.17.cloned.1.call-update) | async-done | bytes 8388624 | tf_op jit(solution)/shard_map/all_gather | solution.py:25
  297.3 8.8 all-reduce.3
  306.2 5.5 convolution_convert_fusion.1
  311.7 3.9 copy.142
  315.7 116.1 %reduce-scatter.7.cloned.1.call-done = bf16[128,512]{1,0:T(8,128)(2,1)} async-done(((bf16[2048,512]{1,0:T(8,128)(2,1)}), bf16[128,512]{1,0:T(8,128)(2,1)}) %reduce-scatter.7.cloned.1.call-update) | async-done | bytes 131088
  433.1 31.8 %all_to_all.10 = bf16[16,512,128]{1,2,0:T(8,128)(2,1)S(1)} all-to-all(bf16[16,512,128]{1,2,0:T(8,128)(2,1)S(1)} %stack.33), channel_id=1, replica_groups=mesh['seq'=16,'wr'=4,'wc'=4] {'wr','wc'}, dimensions={0} | all-to-all | bytes 4194304 | tf_op jit(solution)/shard_map/all_to_all | solution.py:163
  484.4 4.3 exponential_select_fusion.1
  495.3 20.4 %all-gather.13.cloned.1.call-done = bf16[512,1024]{1,0:T(8,128)(2,1)} async-done(((bf16[512,256]{1,0:T(8,128)(2,1)}), bf16[512,1024]{1,0:T(8,128)(2,1)}) %all-gather.13.cloned.1.call-update) | async-done | bytes 1048592 | tf_op jit(solution)/shard_map/all_gather | solution.py:182
  519.0 4.3 fusion.96
  543.7 69.7 %all-reduce.4 = (bf16[16]{0:T(256)(128)(2,1)}, bf16[1,3,256]{2,1,0:T(4,128)(2,1)}, bf16[1,3,256]{2,1,0:T(4,128)(2,1)}, bf16[1,3,256]{2,1,0:T(4,128)(2,1)}, bf16[...) all-reduce(bf16[16]{0:T(256)(128)(2,1)} %dynamic-update-slice.1, ...), channel_id=1, replica_groups=mesh['seq'=16,'wr'=4,'wc'=4] {'seq'}, use_global_device_ids=true, to_apply=%add.1 | all-reduce | flops 4624 | bytes 18496
  618.8 3.3 fusion.52
  622.1 98.3 %all-gather.19.cloned.1.call-done = bf16[16384,256]{1,0:T(8,128)(2,1)} async-done(((bf16[1024,256]{1,0:T(8,128)(2,1)}), bf16[16384,256]{1,0:T(8,128)(2,1)}) %all-gather.19.cloned.1.call-update) | async-done | bytes 8388624 | tf_op jit(solution)/shard_map/all_gather | solution.py:25
  723.8 9.0 all-reduce.2
  732.8 6.1 convolution_convert_fusion
  738.9 3.9 copy.144
  749.3 3.4 fusion.19
  775.1 82.7 %reduce-scatter.9.cloned.1.call-done = bf16[128,512]{1,0:T(8,128)(2,1)} async-done(((bf16[2048,512]{1,0:T(8,128)(2,1)}), bf16[128,512]{1,0:T(8,128)(2,1)}) %reduce-scatter.9.cloned.1.call-update) | async-done | bytes 131088
  859.5 163.8 %all-reduce.8.cloned.1.call-done = (bf16[1,1024,256]{2,1,0:T(8,128)(2,1)}, bf16[1,1024,256]{2,1,0:T(8,128)(2,1)}, bf16[1,1024,256]{2,1,0:T(8,128)(2,1)}, bf16[1,...) async-done(((bf16[1,1024,256]{2,1,0:T(8,128)(2,1)}, bf16[1,1024,256]{2,1,0:T(8,128)(2,1)}, bf16[1,1024,256]{2,1,0:T(8,128)(2,1)}, ...) | async-done | bytes 3145744 | tf_op jit(solution)/shard_map/psum | solution.py:44
  (301 shorter events, 142.8 us)
Async XLA Ops:
  9.7 12.1 %copy-start.43 = (f32[2,4,256]{2,1,0:T(4,128)S(1)}, f32[2,4,256]{2,1,0:T(4,128)}, u32[]{:S(2)}) copy-start(f32[2,4,256]{2,1,0:T(4,128)} %param.26) | copy-start | bytes 24580
  9.7 12.7 %copy-start.36 = (f32[2,2048]{1,0:T(2,128)S(1)}, f32[2,2048]{1,0:T(2,128)}, u32[]{:S(2)}) copy-start(f32[2,2048]{1,0:T(2,128)} %param.21) | copy-start | bytes 49156
  9.7 34.2 %all-to-all-start = ((bf16[16,512,128]{1,2,0:T(8,128)(2,1)}), bf16[16,512,128]{1,2,0:T(8,128)(2,1)S(1)}, u32[]{:S(2)}, u32[]{:S(2)}) async-start(bf16[16,512,128]{1,2,0:T(8,128)(2,1)} %stack.32), calls=%async_computation | async-start | bytes 4194304 | tf_op jit(solution)/shard_map/all_to_all | solution.py:163
  17.3 55.5 %all-gather.11.cloned.1.call-start = ((), (), s32[]{:S(2)}) async-start(), calls=%async_computation.5 | async-start | bytes 1310720 | tf_op jit(solution)/shard_map/all_gather | solution.py:181
  20.0 30.8 %copy-start.51 = (f32[4]{0:T(128)}, f32[4]{0:T(128)S(1)}, u32[]{:S(2)}) copy-start(f32[4]{0:T(128)S(1)} %compare_convert_fusion) | copy-start | bytes 52
  48.0 49.5 %all-gather.9.cloned.1.call-start = ((), (), s32[]{:S(2)}) async-start(), calls=%async_computation.4 | async-start | bytes 1310720 | tf_op jit(solution)/shard_map/all_gather | solution.py:182
  50.9 12.3 %copy-start.31 = (f32[512]{0:T(512)}, f32[512]{0:T(512)S(1)}, u32[]{:S(2)}) copy-start(f32[512]{0:T(512)S(1)} %get-tuple-element.116) | copy-start | bytes 6148
  51.3 5.0 collective-permute-start
  55.9 103.0 %copy-start.24 = (f32[512]{0:T(512)}, f32[512]{0:T(512)S(1)}, u32[]{:S(2)}) copy-start(f32[512]{0:T(512)S(1)} %get-tuple-element.165) | copy-start | bytes 6148
  55.9 103.0 %copy-start.45 = (s32[512]{0:T(512)}, s32[512]{0:T(512)S(1)}, u32[]{:S(2)}) copy-start(s32[512]{0:T(512)S(1)} %convert_add_fusion.2) | copy-start | bytes 6148
  57.5 236.9 %all-gather.17.cloned.1.call-start = ((), (), s32[]{:S(2)}) async-start(), calls=%async_computation.8 | async-start | bytes 8912896 | tf_op jit(solution)/shard_map/all_gather | solution.py:25
  107.4 51.6 %copy-start.4 = (bf16[512,4,256]{2,0,1:T(8,128)(2,1)}, bf16[512,4,256]{2,0,1:T(8,128)(2,1)S(1)}, u32[]{:S(2)}) copy-start(bf16[512,4,256]{2,0,1:T(8,128)(2,1)S(1)} %get-tuple-element.169) | copy-start | bytes 3145732
  111.3 320.4 %reduce-scatter.7.cloned.1.call-start = ((), (), s32[]{:S(2)}) async-start(), calls=%async_computation.10 | async-start | bytes 2228224
  294.5 11.6 %copy-start.2 = (bf16[16,512,128]{1,2,0:T(8,128)(2,1)S(1)}, bf16[16,512,128]{1,2,0:T(8,128)(2,1)}, u32[]{:S(2)}) copy-start(bf16[16,512,128]{1,2,0:T(8,128)(2,1)} %copy-done.1) | copy-start | bytes 6291460
  315.6 117.2 %copy-start.15 = (bf16[512,128]{1,0:T(8,128)(2,1)S(1)}, bf16[512,128]{1,0:T(8,128)(2,1)}, u32[]{:S(2)}) copy-start(bf16[512,128]{1,0:T(8,128)(2,1)} %param.20) | copy-start | bytes 393220
  315.6 175.5 %all-gather.15.cloned.1.call-start = ((), (), s32[]{:S(2)}) async-start(), calls=%async_computation.7 | async-start | bytes 1310720 | tf_op jit(solution)/shard_map/all_gather | solution.py:181
  466.2 13.7 %copy-start = (bf16[16,512,128]{1,2,0:T(8,128)(2,1)}, bf16[16,512,128]{1,2,0:T(8,128)(2,1)S(1)}, u32[]{:S(2)}) copy-start(bf16[16,512,128]{1,2,0:T(8,128)(2,1)S(1)} %fusion.6) | copy-start | bytes 6291460
  468.7 47.0 %all-gather.13.cloned.1.call-start = ((), (), s32[]{:S(2)}) async-start(), calls=%async_computation.6 | async-start | bytes 1310720 | tf_op jit(solution)/shard_map/all_gather | solution.py:182
  469.4 3.8 collective-permute-start.1
  476.7 243.6 %all-gather.19.cloned.1.call-start = ((), (), s32[]{:S(2)}) async-start(), calls=%async_computation.9 | async-start | bytes 8912896 | tf_op jit(solution)/shard_map/all_gather | solution.py:25
  481.1 11.9 %copy-start.35 = (f32[1,1,4,1,256]{4,2,0,1,3:T(4,128)S(1)}, f32[1,1,4,1,256]{4,2,0,1,3:T(4,128)}, u32[]{:S(2)}) copy-start(f32[1,1,4,1,256]{4,2,0,1,3:T(4,128)} %copy.172) | copy-start | bytes 12292
  535.7 322.1 %reduce-scatter.9.cloned.1.call-start = ((), (), s32[]{:S(2)}) async-start(), calls=%async_computation.11 | async-start | bytes 2228224
  618.8 101.6 %copy-start.71 = (bf16[16]{0:T(256)(128)(2,1)S(1)}, bf16[16]{0:T(256)(128)(2,1)}, u32[]{:S(2)}) copy-start(bf16[16]{0:T(256)(128)(2,1)} %get-tuple-element.333) | copy-start | bytes 100
  742.8 280.4 %all-reduce.8.cloned.1.call-start = ((), (), s32[]{:S(2)}) async-start(), calls=%async_computation.12 | async-start | bytes 6291456 | tf_op jit(solution)/shard_map/psum | solution.py:44
  (61 other events, 210.0 us)
Sparse Core Ops, SparseCore 0:
  48.1 24.6 all-gather.10
  74.6 22.8 all-gather.8
  111.4 182.9 all-gather.16
  315.7 115.9 reduce-scatter.6
  468.8 22.3 all-gather.14
  492.8 22.8 all-gather.12
  535.8 184.5 all-gather.18
  743.0 114.7 reduce-scatter.8
  860.9 162.3 all-reduce.7
